TPU v7x, 32 devices: a whole 2x2x4 slice. The times are simulated.
32 devices in a mesh: section: 4 (over y, x), state: 8 (over z, core).
Axes of the slice: x: 2, y: 2, z: 4, core: 2. Of those that a mesh axis runs over, the one named last changes fastest.
Arguments:
- belief: float32 [4, 512, 2048], P('section', None, 'state'), may hold values from 0 to 0.04
- action: int32 [4, 512], P('section'), may hold values from 0 to 7
- next_index: int32 [4, 512, 32], P('section'), may hold values from 0 to 511, as said below
- obs_table: float32 [8, 32, 2048], P(None, None, 'state'), may hold values from -1 to 1
- transition: bfloat16 [8, 2048, 2048], P(None, 'state'), may hold values from -0.1875 to 0.1875
- reward: float32 [8, 2048], P(None, 'state'), may hold values from -6 to 6
- terminal: float32 [512, 2048], P(None, 'state'), may hold values from -6 to 6
Outputs:
- alphas: float32 [4, 512, 2048], P('section', None, 'state')
- values: float32 [4, 512], P('section')
Inputs may be any that keep to these rules, and one draw needn't show every extreme that they name: next_index[h, b, o] < 128 * (b // 128 + 1): a belief of micro-batch m names only next-section alpha vectors of micro-batches 0 to m.
All inputs are finite; a program needn't handle non-finite values.
Results may differ from a plain program's by a relative error of at most 0.012.
Values sent between devices are 32-bit elements; how exact they have to be, the bound alone decides.
No kernel may reach another device: no remote copies, remote signals or barrier semaphores. Data moves between devices by JAX's collectives and lax.ppermute only.
A program may use at most 64 MiB of HBM per device.

v0:
```python
import jax
import jax.numpy as jnp
from jax import lax
from jax.sharding import PartitionSpec as P

discount = 0.95


def backup(next_alphas, act_rows, next_rows, belief_rows, obs_table, transition, reward):
    actions = obs_table.shape[0]
    local_width = obs_table.shape[2]
    row_count = act_rows.shape[0]
    picked = next_alphas[next_rows]
    per_action = jnp.einsum("bos,aos->bas", picked, obs_table, precision=lax.Precision.HIGHEST)
    onehot = (act_rows[:, None] == jnp.arange(actions, dtype=jnp.int32)[None, :]).astype(
        jnp.float32
    )
    masked = (
        (per_action * onehot[:, :, None])
        .astype(jnp.bfloat16)
        .reshape(row_count, actions * local_width)
    )
    trans_flat = transition.reshape(actions * local_width, transition.shape[2])
    partial_value = jnp.dot(masked, trans_flat, preferred_element_type=jnp.float32)
    summed = lax.psum_scatter(partial_value, "state", scatter_dimension=1, tiled=True)
    reward_rows = jnp.dot(onehot, reward, precision=lax.Precision.HIGHEST)
    section_alphas = reward_rows + discount * summed
    section_values = lax.psum(jnp.sum(belief_rows * section_alphas, axis=1), "state")
    return (section_alphas, section_values)


def local(belief, action, next_index, obs_table, transition, reward, terminal):
    section_index = lax.axis_index("section")
    sections = lax.axis_size("section")
    beliefs = terminal.shape[0]
    local_width = terminal.shape[1]
    share = beliefs // sections
    every_action, every_next = (
        lax.all_gather(action, "section", axis=0, tiled=True),
        lax.all_gather(next_index, "section", axis=0, tiled=True),
    )
    shared_belief = lax.all_to_all(belief, "section", split_axis=1, concat_axis=0, tiled=True)
    offset = section_index * share

    def turn(turn_number, carry):
        nextset, kept_alphas, kept_values = carry
        horizon_step = (sections - 1 - turn_number).astype(jnp.int32)
        act_section = lax.dynamic_index_in_dim(every_action, horizon_step, 0, False)
        next_section_rows = lax.dynamic_index_in_dim(every_next, horizon_step, 0, False)
        act_rows = lax.dynamic_slice_in_dim(act_section, offset, share, 0)
        next_rows = lax.dynamic_slice_in_dim(next_section_rows, offset, share, 0)
        belief_rows = lax.dynamic_index_in_dim(shared_belief, horizon_step, 0, False)
        part_alphas, part_values = backup(
            nextset, act_rows, next_rows, belief_rows, obs_table, transition, reward
        )
        nextset = lax.all_gather(part_alphas, "section", axis=0, tiled=True)
        kept_alphas = lax.dynamic_update_index_in_dim(kept_alphas, part_alphas, horizon_step, 0)
        kept_values = lax.dynamic_update_index_in_dim(kept_values, part_values, horizon_step, 0)
        return (nextset, kept_alphas, kept_values)

    start = (
        terminal,
        jnp.zeros((sections, share, local_width), jnp.float32),
        jnp.zeros((sections, share), jnp.float32),
    )
    result = lax.fori_loop(0, sections, turn, start)
    out_alphas, out_values = (
        lax.all_to_all(result[1], "section", split_axis=0, concat_axis=1, tiled=True),
        lax.all_to_all(result[2], "section", split_axis=0, concat_axis=1, tiled=True),
    )
    return (out_alphas, out_values)


def solution(mesh):
    return jax.shard_map(
        local,
        mesh=mesh,
        in_specs=(
            P("section", None, "state"),
            P("section", None),
            P("section", None, None),
            P(None, None, "state"),
            P(None, "state", None),
            P(None, "state"),
            P(None, "state"),
        ),
        out_specs=(P("section", None, "state"), P("section", None)),
        check_vma=False,
    )
```

profile of v0, /device:TPU:0, one launch (start us, length us, event | category | flops | bytes accessed | tf_op | source)
XLA Modules:
  0.0 433.7 jit_solution(1737412535606526940)
XLA Ops:
  7.2 2.4 copy.17
  9.5 5.2 %all-to-all-start = ((f32[1,512,256]{2,0,1:T(1,128)}), f32[1,512,256]{2,0,1:T(1,128)S(1)}, u32[]{:S(2)}, u32[]{:S(2)}) async-start(f32[1,512,256]{2,0,1:T(1,128)} %copy.17), calls=%async_computation.1 | async-start | bytes 1048576 | tf_op jit(solution)/shard_map/all_to_all | solution.py:42
  14.7 11.2 %all-gather = s32[4,1,512]{2,1,0:T(1,128)S(1)} all-gather(s32[1,1,512]{2,1,0:T(1,128)} %bitcast.64), channel_id=1, replica_groups=mesh['section'=4,'state'=8] {'section'}, dimensions={0}, use_global_device_ids=true | all-gather | bytes 10240 | tf_op jit(solution)/shard_map/all_gather | solution.py:39
  25.9 1.4 copy.19
  27.4 11.3 %copy.20 = bf16[8,256,2048]{2,0,1:T(8,128)(2,1)} copy(bf16[8,256,2048]{2,1,0:T(8,128)(2,1)} %param.13) | data formatting | bytes 16777216 | tf_op jit(solution)/shard_map/while | solution.py:66
  38.7 8.0 %all_gather.18 = s32[4,512,32]{1,2,0:T(8,128)S(1)} all-gather(s32[1,512,32]{1,2,0:T(8,128)S(1)} %copy-done.2), channel_id=1, replica_groups=mesh['section'=4,'state'=8] {'section'}, dimensions={0}, use_global_device_ids=true | all-gather | bytes 327680 | tf_op jit(solution)/shard_map/all_gather | solution.py:40
  46.7 0.8 broadcast_in_dim.42
  47.6 360.7 %while.20 = (s32[]{:T(128)}, f32[512,256]{1,0:T(8,128)S(1)}, f32[4,128,256]{2,1,0:T(8,128)}, f32[4,128]{1,0:T(4,128)S(1)}, s32[4,512]{1,0:T(4,128)S(1)}, /*index...) while((s32[]{:T(128)}, f32[512,256]{1,0:T(8,128)S(1)}, ...), condition=%wide.region_4.5_spmd, body=%wide.region_0.4_spmd.sunk | while | flops 1178225664 | bytes 36770572 | solution.py:66
  47.9 16.1 %gather_fusion = f32[4096,256]{1,0:T(8,128)} fusion(f32[512,256]{1,0:T(8,128)S(1)} %get-tuple-element.453, s32[4096]{0:T(1024)S(1)} %broadcast_clamp_fusion.2), kind=kCustom, calls=%fused_computation.clone.1 | custom fusion | bytes 8404992 | tf_op jit(solution)/shard_map/while/body/eval_jaxpr/gather | solution.py:13
  64.0 5.9 %copy.29 = f32[128,32,256]{0,1,2:T(8,128)} copy(f32[128,32,256]{2,1,0:T(8,128)} %bitcast.57) | data formatting | bytes 8388608 | tf_op jit(solution)/shard_map/while/body/eval_jaxpr/gather | solution.py:13
  70.0 5.5 %fusion.24 = bf16[128,8,256]{0,1,2:T(8,128)(2,1)S(1)} fusion(f32[128,32,256]{0,1,2:T(8,128)} %copy.29, f32[8,32,256]{1,0,2:T(8,128)S(1)} %get-tuple-element.475, f32[128,8]{0,1:T(8,128)S(1)} %fusion.23), kind=kOutput, calls=%fused_computation.4.clone.1 | convolution fusion | flops 101187584 | bytes 4984832 | tf_op jit(solution)/shard_map/while/body/eval_jaxpr/bos,aos->bas/dot_general | solution.py:14
  75.5 5.8 %convolution_bitcast_fusion.2 = f32[128,2048]{1,0:T(8,128)} fusion(bf16[128,8,256]{0,1,2:T(8,128)(2,1)S(1)} %fusion.24, bf16[8,256,2048]{2,0,1:T(8,128)(2,1)} %get-tuple-element.476), kind=kOutput, calls=%fused_computation.1.clone.1 | convolution fusion | flops 1073741824 | bytes 9961472 | tf_op jit(solution)/shard_map/while/body/eval_jaxpr/dot_general | solution.py:24
  81.3 33.0 %reduce-scatter.2.cloned.1.call-done = f32[128,256]{1,0:T(8,128)} async-done(((f32[128,2048]{1,0:T(8,128)}), f32[128,256]{1,0:T(8,128)}) %reduce-scatter.2.cloned.1.call-update) | async-done | bytes 131088 | tf_op jit(solution)/shard_map/while/body/eval_jaxpr/reduce_scatter | solution.py:25
  114.3 1.8 bitcast_dynamic-update-slice_fusion.2
  116.1 10.1 %all_gather.20 = f32[512,256]{1,0:T(8,128)S(1)} all-gather(f32[128,256]{1,0:T(8,128)S(1)} %get-tuple-element.435), channel_id=1, replica_groups=mesh['section'=4,'state'=8] {'section'}, dimensions={0}, use_global_device_ids=true | all-gather | bytes 655360 | tf_op jit(solution)/shard_map/while/body/eval_jaxpr/all_gather | solution.py:56
  126.2 0.1 fusion.25
  126.3 13.7 %psum.16 = f32[1,128]{1,0:T(1,128)S(1)} all-reduce(f32[1,128]{1,0:T(1,128)S(1)} %bitcast.61), channel_id=1, replica_groups=mesh['section'=4,'state'=8] {'state'}, use_global_device_ids=true, to_apply=%region_3.3 | all-reduce | flops 128 | bytes 1024 | tf_op jit(solution)/shard_map/while/body/eval_jaxpr/psum | solution.py:28
  140.4 16.1 %gather_fusion = f32[4096,256]{1,0:T(8,128)} fusion(f32[512,256]{1,0:T(8,128)S(1)} %get-tuple-element.453, s32[4096]{0:T(1024)S(1)} %broadcast_clamp_fusion.2), kind=kCustom, calls=%fused_computation.clone.1 | custom fusion | bytes 8404992 | tf_op jit(solution)/shard_map/while/body/eval_jaxpr/gather | solution.py:13
  156.5 5.9 %copy.29 = f32[128,32,256]{0,1,2:T(8,128)} copy(f32[128,32,256]{2,1,0:T(8,128)} %bitcast.57) | data formatting | bytes 8388608 | tf_op jit(solution)/shard_map/while/body/eval_jaxpr/gather | solution.py:13
  162.5 5.5 %fusion.24 = bf16[128,8,256]{0,1,2:T(8,128)(2,1)S(1)} fusion(f32[128,32,256]{0,1,2:T(8,128)} %copy.29, f32[8,32,256]{1,0,2:T(8,128)S(1)} %get-tuple-element.475, f32[128,8]{0,1:T(8,128)S(1)} %fusion.23), kind=kOutput, calls=%fused_computation.4.clone.1 | convolution fusion | flops 101187584 | bytes 4984832 | tf_op jit(solution)/shard_map/while/body/eval_jaxpr/bos,aos->bas/dot_general | solution.py:14
  168.0 5.8 %convolution_bitcast_fusion.2 = f32[128,2048]{1,0:T(8,128)} fusion(bf16[128,8,256]{0,1,2:T(8,128)(2,1)S(1)} %fusion.24, bf16[8,256,2048]{2,0,1:T(8,128)(2,1)} %get-tuple-element.476), kind=kOutput, calls=%fused_computation.1.clone.1 | convolution fusion | flops 1073741824 | bytes 9961472 | tf_op jit(solution)/shard_map/while/body/eval_jaxpr/dot_general | solution.py:24
  173.8 30.0 %reduce-scatter.2.cloned.1.call-done = f32[128,256]{1,0:T(8,128)} async-done(((f32[128,2048]{1,0:T(8,128)}), f32[128,256]{1,0:T(8,128)}) %reduce-scatter.2.cloned.1.call-update) | async-done | bytes 131088 | tf_op jit(solution)/shard_map/while/body/eval_jaxpr/reduce_scatter | solution.py:25
  203.7 1.8 bitcast_dynamic-update-slice_fusion.2
  205.6 10.0 %all_gather.20 = f32[512,256]{1,0:T(8,128)S(1)} all-gather(f32[128,256]{1,0:T(8,128)S(1)} %get-tuple-element.435), channel_id=1, replica_groups=mesh['section'=4,'state'=8] {'section'}, dimensions={0}, use_global_device_ids=true | all-gather | bytes 655360 | tf_op jit(solution)/shard_map/while/body/eval_jaxpr/all_gather | solution.py:56
  215.6 0.1 fusion.25
  215.7 13.7 %psum.16 = f32[1,128]{1,0:T(1,128)S(1)} all-reduce(f32[1,128]{1,0:T(1,128)S(1)} %bitcast.61), channel_id=1, replica_groups=mesh['section'=4,'state'=8] {'state'}, use_global_device_ids=true, to_apply=%region_3.3 | all-reduce | flops 128 | bytes 1024 | tf_op jit(solution)/shard_map/while/body/eval_jaxpr/psum | solution.py:28
  229.8 16.1 %gather_fusion = f32[4096,256]{1,0:T(8,128)} fusion(f32[512,256]{1,0:T(8,128)S(1)} %get-tuple-element.453, s32[4096]{0:T(1024)S(1)} %broadcast_clamp_fusion.2), kind=kCustom, calls=%fused_computation.clone.1 | custom fusion | bytes 8404992 | tf_op jit(solution)/shard_map/while/body/eval_jaxpr/gather | solution.py:13
  245.9 5.9 %copy.29 = f32[128,32,256]{0,1,2:T(8,128)} copy(f32[128,32,256]{2,1,0:T(8,128)} %bitcast.57) | data formatting | bytes 8388608 | tf_op jit(solution)/shard_map/while/body/eval_jaxpr/gather | solution.py:13
  251.9 5.5 %fusion.24 = bf16[128,8,256]{0,1,2:T(8,128)(2,1)S(1)} fusion(f32[128,32,256]{0,1,2:T(8,128)} %copy.29, f32[8,32,256]{1,0,2:T(8,128)S(1)} %get-tuple-element.475, f32[128,8]{0,1:T(8,128)S(1)} %fusion.23), kind=kOutput, calls=%fused_computation.4.clone.1 | convolution fusion | flops 101187584 | bytes 4984832 | tf_op jit(solution)/shard_map/while/body/eval_jaxpr/bos,aos->bas/dot_general | solution.py:14
  257.3 5.8 %convolution_bitcast_fusion.2 = f32[128,2048]{1,0:T(8,128)} fusion(bf16[128,8,256]{0,1,2:T(8,128)(2,1)S(1)} %fusion.24, bf16[8,256,2048]{2,0,1:T(8,128)(2,1)} %get-tuple-element.476), kind=kOutput, calls=%fused_computation.1.clone.1 | convolution fusion | flops 1073741824 | bytes 9961472 | tf_op jit(solution)/shard_map/while/body/eval_jaxpr/dot_general | solution.py:24
  263.1 30.0 %reduce-scatter.2.cloned.1.call-done = f32[128,256]{1,0:T(8,128)} async-done(((f32[128,2048]{1,0:T(8,128)}), f32[128,256]{1,0:T(8,128)}) %reduce-scatter.2.cloned.1.call-update) | async-done | bytes 131088 | tf_op jit(solution)/shard_map/while/body/eval_jaxpr/reduce_scatter | solution.py:25
  293.2 1.8 bitcast_dynamic-update-slice_fusion.2
  295.0 10.0 %all_gather.20 = f32[512,256]{1,0:T(8,128)S(1)} all-gather(f32[128,256]{1,0:T(8,128)S(1)} %get-tuple-element.435), channel_id=1, replica_groups=mesh['section'=4,'state'=8] {'section'}, dimensions={0}, use_global_device_ids=true | all-gather | bytes 655360 | tf_op jit(solution)/shard_map/while/body/eval_jaxpr/all_gather | solution.py:56
  305.1 13.7 %psum.16 = f32[1,128]{1,0:T(1,128)S(1)} all-reduce(f32[1,128]{1,0:T(1,128)S(1)} %bitcast.61), channel_id=1, replica_groups=mesh['section'=4,'state'=8] {'state'}, use_global_device_ids=true, to_apply=%region_3.3 | all-reduce | flops 128 | bytes 1024 | tf_op jit(solution)/shard_map/while/body/eval_jaxpr/psum | solution.py:28
  319.1 16.1 %gather_fusion = f32[4096,256]{1,0:T(8,128)} fusion(f32[512,256]{1,0:T(8,128)S(1)} %get-tuple-element.453, s32[4096]{0:T(1024)S(1)} %broadcast_clamp_fusion.2), kind=kCustom, calls=%fused_computation.clone.1 | custom fusion | bytes 8404992 | tf_op jit(solution)/shard_map/while/body/eval_jaxpr/gather | solution.py:13
  335.2 5.9 %copy.29 = f32[128,32,256]{0,1,2:T(8,128)} copy(f32[128,32,256]{2,1,0:T(8,128)} %bitcast.57) | data formatting | bytes 8388608 | tf_op jit(solution)/shard_map/while/body/eval_jaxpr/gather | solution.py:13
  341.2 5.5 %fusion.24 = bf16[128,8,256]{0,1,2:T(8,128)(2,1)S(1)} fusion(f32[128,32,256]{0,1,2:T(8,128)} %copy.29, f32[8,32,256]{1,0,2:T(8,128)S(1)} %get-tuple-element.475, f32[128,8]{0,1:T(8,128)S(1)} %fusion.23), kind=kOutput, calls=%fused_computation.4.clone.1 | convolution fusion | flops 101187584 | bytes 4984832 | tf_op jit(solution)/shard_map/while/body/eval_jaxpr/bos,aos->bas/dot_general | solution.py:14
  346.7 5.8 %convolution_bitcast_fusion.2 = f32[128,2048]{1,0:T(8,128)} fusion(bf16[128,8,256]{0,1,2:T(8,128)(2,1)S(1)} %fusion.24, bf16[8,256,2048]{2,0,1:T(8,128)(2,1)} %get-tuple-element.476), kind=kOutput, calls=%fused_computation.1.clone.1 | convolution fusion | flops 1073741824 | bytes 9961472 | tf_op jit(solution)/shard_map/while/body/eval_jaxpr/dot_general | solution.py:24
  352.5 30.1 %reduce-scatter.2.cloned.1.call-done = f32[128,256]{1,0:T(8,128)} async-done(((f32[128,2048]{1,0:T(8,128)}), f32[128,256]{1,0:T(8,128)}) %reduce-scatter.2.cloned.1.call-update) | async-done | bytes 131088 | tf_op jit(solution)/shard_map/while/body/eval_jaxpr/reduce_scatter | solution.py:25
  382.6 1.8 bitcast_dynamic-update-slice_fusion.2
  384.4 10.0 %all_gather.20 = f32[512,256]{1,0:T(8,128)S(1)} all-gather(f32[128,256]{1,0:T(8,128)S(1)} %get-tuple-element.435), channel_id=1, replica_groups=mesh['section'=4,'state'=8] {'section'}, dimensions={0}, use_global_device_ids=true | all-gather | bytes 655360 | tf_op jit(solution)/shard_map/while/body/eval_jaxpr/all_gather | solution.py:56
  394.4 0.1 fusion.25
  394.5 13.7 %psum.16 = f32[1,128]{1,0:T(1,128)S(1)} all-reduce(f32[1,128]{1,0:T(1,128)S(1)} %bitcast.61), channel_id=1, replica_groups=mesh['section'=4,'state'=8] {'state'}, use_global_device_ids=true, to_apply=%region_3.3 | all-reduce | flops 128 | bytes 1024 | tf_op jit(solution)/shard_map/while/body/eval_jaxpr/psum | solution.py:28
  408.2 7.2 %all_to_all.40 = f32[4,1,128]{2,1,0:T(1,128)S(1)} all-to-all(f32[4,1,128]{2,1,0:T(1,128)S(1)} %bitcast.62), channel_id=1, replica_groups=mesh['section'=4,'state'=8] {'section'}, dimensions={0} | all-to-all | bytes 4096 | tf_op jit(solution)/shard_map/all_to_all | solution.py:69
  415.4 3.5 all-to-all-start.1
  418.9 6.9 %all-to-all-done.1 = f32[4,128,256]{2,1,0:T(8,128)S(1)} async-done(((f32[4,128,256]{2,1,0:T(8,128)}), f32[4,128,256]{2,1,0:T(8,128)S(1)}, u32[]{:S(2)}, u32[]{:S(2)}) %all-to-all-start.1) | async-done | bytes 524320 | tf_op jit(solution)/shard_map/all_to_all | solution.py:68
  425.8 0.8 copy.48
  426.6 0.6 copy.49
  (51 shorter events, 2.0 us)
Async XLA Ops:
  9.5 37.1 %all-to-all-start = ((f32[1,512,256]{2,0,1:T(1,128)}), f32[1,512,256]{2,0,1:T(1,128)S(1)}, u32[]{:S(2)}, u32[]{:S(2)}) async-start(f32[1,512,256]{2,0,1:T(1,128)} %copy.17), calls=%async_computation.1 | async-start | bytes 1048576 | tf_op jit(solution)/shard_map/all_to_all | solution.py:42
  27.3 11.3 %copy-start.2 = (s32[1,512,32]{1,2,0:T(8,128)S(1)}, s32[1,512,32]{1,2,0:T(8,128)}, u32[]{:S(2)}) copy-start(s32[1,512,32]{1,2,0:T(8,128)} %param.11) | copy-start | bytes 196612
  27.3 20.2 %copy-start = (f32[512,256]{1,0:T(8,128)S(1)}, f32[512,256]{1,0:T(8,128)}, u32[]{:S(2)}) copy-start(f32[512,256]{1,0:T(8,128)} %param.15) | copy-start | bytes 1572868
  27.3 20.2 %copy-start.1 = (f32[8,256]{1,0:T(8,128)S(1)}, f32[8,256]{1,0:T(8,128)}, u32[]{:S(2)}) copy-start(f32[8,256]{1,0:T(8,128)} %param.14) | copy-start | bytes 24580
  47.6 66.7 %reduce-scatter.2.cloned.1.call-start = ((), (), s32[]{:S(2)}) async-start(), calls=%async_computation.4 | async-start | bytes 1179648 | tf_op jit(solution)/shard_map/while/body/eval_jaxpr/reduce_scatter | solution.py:25
  140.0 63.7 %reduce-scatter.2.cloned.1.call-start = ((), (), s32[]{:S(2)}) async-start(), calls=%async_computation.4 | async-start | bytes 1179648 | tf_op jit(solution)/shard_map/while/body/eval_jaxpr/reduce_scatter | solution.py:25
  229.4 63.8 %reduce-scatter.2.cloned.1.call-start = ((), (), s32[]{:S(2)}) async-start(), calls=%async_computation.4 | async-start | bytes 1179648 | tf_op jit(solution)/shard_map/while/body/eval_jaxpr/reduce_scatter | solution.py:25
  318.8 63.8 %reduce-scatter.2.cloned.1.call-start = ((), (), s32[]{:S(2)}) async-start(), calls=%async_computation.4 | async-start | bytes 1179648 | tf_op jit(solution)/shard_map/while/body/eval_jaxpr/reduce_scatter | solution.py:25
  415.4 10.4 %all-to-all-start.1 = ((f32[4,128,256]{2,1,0:T(8,128)}), f32[4,128,256]{2,1,0:T(8,128)S(1)}, u32[]{:S(2)}, u32[]{:S(2)}) async-start(f32[4,128,256]{2,1,0:T(8,128)} %get-tuple-element.318), calls=%async_computation.2 | async-start | bytes 1048576 | tf_op jit(solution)/shard_map/all_to_all | solution.py:68
Sparse Core Ops, SparseCore 0:
  81.4 32.8 reduce-scatter.1
  173.9 29.8 reduce-scatter.1
  263.3 29.8 reduce-scatter.1
  352.6 29.8 reduce-scatter.1
where the time goes:
time: 435 us; the launch traced here: 434 us
  waiting for transfers between devices  130 us (30%)
  blocking collectives  121 us (28%)
  local copies, waits for them, and re-layouts  107 us (25%)
  matrix products  52.2 us (12%)
  between operations  13.8 us (3%)
  starting transfers between devices  8.82 us (2%)
    reduce_scatter x4, waiting for transfers between devices, backup(): lax.psum_scatter(partial_value, 'state', scatter_dimension=1, tiled=True)  123 us
    gather x8, local copies, waits for them, and re-layouts, backup(): picked = next_alphas[next_rows]  88.1 us
    psum x4, blocking collectives, backup(): lax.psum(jnp.sum(belief_rows * section_alphas, axis=1), 'state')  54.7 us
    all_gather x4, blocking collectives, turn(): nextset = lax.all_gather(part_alphas, 'section', axis=0, tiled=True)  40.1 us
    dot_general x4, matrix products, backup(): jnp.dot(masked, trans_flat, preferred_element_type=jnp.float32)  23.1 us
    dot_general x4, matrix products, backup(): jnp.einsum('bos,aos->bas', picked, obs_table, precision=lax.Precision.HIG...  21.9 us
    while x2, local copies, waits for them, and re-layouts, local(): result = lax.fori_loop(0, sections, turn, start)  12.7 us
    all_gather x1, blocking collectives, local(): lax.all_gather(action, 'section', axis=0, tiled=True)  11.2 us
  transfers between devices with their start and end apart: 6, of which 5 were waited for; matrix products, arithmetic and copies ran while one was open for 3% of the time, Pallas kernels for 0%

commit v1 on v0

--- a/solution.py
+++ b/solution.py
@@ -25,7 +25,9 @@
     summed = lax.psum_scatter(partial_value, "state", scatter_dimension=1, tiled=True)
     reward_rows = jnp.dot(onehot, reward, precision=lax.Precision.HIGHEST)
     section_alphas = reward_rows + discount * summed
-    section_values = lax.psum(jnp.sum(belief_rows * section_alphas, axis=1), "state")
+    section_values = jnp.sum(
+        lax.all_gather(jnp.sum(belief_rows * section_alphas, axis=1), "state"), axis=0
+    )
     return (section_alphas, section_values)
 
 

time: 435 us -> 420 us (0.966)
  blocking collectives: 121 us -> 104 us
    psum x4 -> x0, blocking collectives: 54.7 us -> none  [backup(): lax.psum(jnp.sum(belief_rows * section_alphas, axis=1), 'state')]
    all_gather x0 -> x4, blocking collectives: none -> 37.4 us  [backup(): lax.all_gather(jnp.sum(belief_rows * section_alphas, axis=1), 'state')]
where the time goes in v1:
time: 420 us; the launch traced here: 419 us
  waiting for transfers between devices  132 us (31%)
  local copies, waits for them, and re-layouts  107 us (25%)
  blocking collectives  104 us (25%)
  matrix products  52.2 us (12%)
  between operations  13.8 us (3%)
  starting transfers between devices  8.82 us (2%)
    reduce_scatter x4, waiting for transfers between devices, backup(): lax.psum_scatter(partial_value, 'state', scatter_dimension=1, tiled=True)  124 us
    gather x8, local copies, waits for them, and re-layouts, backup(): picked = next_alphas[next_rows]  88.1 us
    all_gather x4, blocking collectives, turn(): nextset = lax.all_gather(part_alphas, 'section', axis=0, tiled=True)  40.4 us
    all_gather x4, blocking collectives, backup(): lax.all_gather(jnp.sum(belief_rows * section_alphas, axis=1), 'state')  37.4 us
    dot_general x4, matrix products, backup(): jnp.dot(masked, trans_flat, preferred_element_type=jnp.float32)  23.1 us
    dot_general x4, matrix products, backup(): jnp.einsum('bos,aos->bas', picked, obs_table, precision=lax.Precision.HIG...  21.9 us
    while x2, local copies, waits for them, and re-layouts, local(): result = lax.fori_loop(0, sections, turn, start)  12.7 us
    all_gather x1, blocking collectives, local(): lax.all_gather(action, 'section', axis=0, tiled=True)  11.2 us
  transfers between devices with their start and end apart: 6, of which 5 were waited for; matrix products, arithmetic and copies ran while one was open for 3% of the time, Pallas kernels for 0%

profile of v1, /device:TPU:0, one launch (start us, length us, event | category | flops | bytes accessed | tf_op | source)
XLA Modules:
  0.0 418.7 jit_solution(4748796631810239418)
XLA Ops:
  7.2 2.4 copy.17
  9.5 5.2 %all-to-all-start = ((f32[1,512,256]{2,0,1:T(1,128)}), f32[1,512,256]{2,0,1:T(1,128)S(1)}, u32[]{:S(2)}, u32[]{:S(2)}) async-start(f32[1,512,256]{2,0,1:T(1,128)} %copy.17), calls=%async_computation.1 | async-start | bytes 1048576 | tf_op jit(solution)/shard_map/all_to_all | solution.py:44
  14.7 11.2 %all-gather.2 = s32[4,1,512]{2,1,0:T(1,128)S(1)} all-gather(s32[1,1,512]{2,1,0:T(1,128)} %bitcast.68), channel_id=1, replica_groups=mesh['section'=4,'state'=8] {'section'}, dimensions={0}, use_global_device_ids=true | all-gather | bytes 10240 | tf_op jit(solution)/shard_map/all_gather | solution.py:41
  25.9 1.4 copy.19
  27.4 11.3 %copy.20 = bf16[8,256,2048]{2,0,1:T(8,128)(2,1)} copy(bf16[8,256,2048]{2,1,0:T(8,128)(2,1)} %param.13) | data formatting | bytes 16777216 | tf_op jit(solution)/shard_map/while | solution.py:68
  38.7 8.0 %all_gather.40 = s32[4,512,32]{1,2,0:T(8,128)S(1)} all-gather(s32[1,512,32]{1,2,0:T(8,128)S(1)} %copy-done.2), channel_id=1, replica_groups=mesh['section'=4,'state'=8] {'section'}, dimensions={0}, use_global_device_ids=true | all-gather | bytes 327680 | tf_op jit(solution)/shard_map/all_gather | solution.py:42
  46.7 0.8 broadcast_in_dim.42
  47.6 345.1 %while.20 = (s32[]{:T(128)}, f32[512,256]{1,0:T(8,128)S(1)}, f32[4,128,256]{2,1,0:T(8,128)}, f32[4,128]{1,0:T(4,128)S(1)}, s32[4,512]{1,0:T(4,128)S(1)}, /*index...) while((s32[]{:T(128)}, f32[512,256]{1,0:T(8,128)S(1)}, ...), condition=%wide.region_4.5_spmd, body=%wide.region_0.4_spmd.sunk | while | flops 1178226432 | bytes 36778776 | solution.py:68
  47.9 16.1 %gather_fusion = f32[4096,256]{1,0:T(8,128)} fusion(f32[512,256]{1,0:T(8,128)S(1)} %get-tuple-element.454, s32[4096]{0:T(1024)S(1)} %broadcast_clamp_fusion.2), kind=kCustom, calls=%fused_computation.clone.1 | custom fusion | bytes 8404992 | tf_op jit(solution)/shard_map/while/body/eval_jaxpr/gather | solution.py:13
  64.0 5.9 %copy.29 = f32[128,32,256]{0,1,2:T(8,128)} copy(f32[128,32,256]{2,1,0:T(8,128)} %bitcast.60) | data formatting | bytes 8388608 | tf_op jit(solution)/shard_map/while/body/eval_jaxpr/gather | solution.py:13
  70.0 5.5 %fusion.24 = bf16[128,8,256]{0,1,2:T(8,128)(2,1)S(1)} fusion(f32[128,32,256]{0,1,2:T(8,128)} %copy.29, f32[8,32,256]{1,0,2:T(8,128)S(1)} %get-tuple-element.477, f32[128,8]{0,1:T(8,128)S(1)} %fusion.23), kind=kOutput, calls=%fused_computation.4.clone.1 | convolution fusion | flops 101187584 | bytes 4984832 | tf_op jit(solution)/shard_map/while/body/eval_jaxpr/bos,aos->bas/dot_general | solution.py:14
  75.5 5.8 %convolution_bitcast_fusion.2 = f32[128,2048]{1,0:T(8,128)} fusion(bf16[128,8,256]{0,1,2:T(8,128)(2,1)S(1)} %fusion.24, bf16[8,256,2048]{2,0,1:T(8,128)(2,1)} %get-tuple-element.478), kind=kOutput, calls=%fused_computation.1.clone.1 | convolution fusion | flops 1073741824 | bytes 9961472 | tf_op jit(solution)/shard_map/while/body/eval_jaxpr/dot_general | solution.py:24
  81.3 33.0 %reduce-scatter.2.cloned.1.call-done = f32[128,256]{1,0:T(8,128)} async-done(((f32[128,2048]{1,0:T(8,128)}), f32[128,256]{1,0:T(8,128)}) %reduce-scatter.2.cloned.1.call-update) | async-done | bytes 131088 | tf_op jit(solution)/shard_map/while/body/eval_jaxpr/reduce_scatter | solution.py:25
  114.3 1.8 bitcast_dynamic-update-slice_fusion.2
  116.1 10.1 %all_gather.42 = f32[512,256]{1,0:T(8,128)S(1)} all-gather(f32[128,256]{1,0:T(8,128)S(1)} %get-tuple-element.435), channel_id=1, replica_groups=mesh['section'=4,'state'=8] {'section'}, dimensions={0}, use_global_device_ids=true | all-gather | bytes 655360 | tf_op jit(solution)/shard_map/while/body/eval_jaxpr/all_gather | solution.py:58
  126.2 0.1 fusion.25
  126.3 9.3 %all-gather.4 = f32[8,1,128]{2,1,0:T(1,128)S(1)} all-gather(f32[1,1,128]{2,1,0:T(1,128)S(1)} %bitcast.63), channel_id=2, replica_groups=mesh['section'=4,'state'=8] {'state'}, dimensions={0}, use_global_device_ids=true | all-gather | bytes 4608 | tf_op jit(solution)/shard_map/while/body/eval_jaxpr/all_gather | solution.py:29
  136.1 16.1 %gather_fusion = f32[4096,256]{1,0:T(8,128)} fusion(f32[512,256]{1,0:T(8,128)S(1)} %get-tuple-element.454, s32[4096]{0:T(1024)S(1)} %broadcast_clamp_fusion.2), kind=kCustom, calls=%fused_computation.clone.1 | custom fusion | bytes 8404992 | tf_op jit(solution)/shard_map/while/body/eval_jaxpr/gather | solution.py:13
  152.2 5.9 %copy.29 = f32[128,32,256]{0,1,2:T(8,128)} copy(f32[128,32,256]{2,1,0:T(8,128)} %bitcast.60) | data formatting | bytes 8388608 | tf_op jit(solution)/shard_map/while/body/eval_jaxpr/gather | solution.py:13
  158.2 5.5 %fusion.24 = bf16[128,8,256]{0,1,2:T(8,128)(2,1)S(1)} fusion(f32[128,32,256]{0,1,2:T(8,128)} %copy.29, f32[8,32,256]{1,0,2:T(8,128)S(1)} %get-tuple-element.477, f32[128,8]{0,1:T(8,128)S(1)} %fusion.23), kind=kOutput, calls=%fused_computation.4.clone.1 | convolution fusion | flops 101187584 | bytes 4984832 | tf_op jit(solution)/shard_map/while/body/eval_jaxpr/bos,aos->bas/dot_general | solution.py:14
  163.6 5.8 %convolution_bitcast_fusion.2 = f32[128,2048]{1,0:T(8,128)} fusion(bf16[128,8,256]{0,1,2:T(8,128)(2,1)S(1)} %fusion.24, bf16[8,256,2048]{2,0,1:T(8,128)(2,1)} %get-tuple-element.478), kind=kOutput, calls=%fused_computation.1.clone.1 | convolution fusion | flops 1073741824 | bytes 9961472 | tf_op jit(solution)/shard_map/while/body/eval_jaxpr/dot_general | solution.py:24
  169.4 30.5 %reduce-scatter.2.cloned.1.call-done = f32[128,256]{1,0:T(8,128)} async-done(((f32[128,2048]{1,0:T(8,128)}), f32[128,256]{1,0:T(8,128)}) %reduce-scatter.2.cloned.1.call-update) | async-done | bytes 131088 | tf_op jit(solution)/shard_map/while/body/eval_jaxpr/reduce_scatter | solution.py:25
  199.9 1.8 bitcast_dynamic-update-slice_fusion.2
  201.7 10.1 %all_gather.42 = f32[512,256]{1,0:T(8,128)S(1)} all-gather(f32[128,256]{1,0:T(8,128)S(1)} %get-tuple-element.435), channel_id=1, replica_groups=mesh['section'=4,'state'=8] {'section'}, dimensions={0}, use_global_device_ids=true | all-gather | bytes 655360 | tf_op jit(solution)/shard_map/while/body/eval_jaxpr/all_gather | solution.py:58
  211.9 9.4 %all-gather.4 = f32[8,1,128]{2,1,0:T(1,128)S(1)} all-gather(f32[1,1,128]{2,1,0:T(1,128)S(1)} %bitcast.63), channel_id=2, replica_groups=mesh['section'=4,'state'=8] {'state'}, dimensions={0}, use_global_device_ids=true | all-gather | bytes 4608 | tf_op jit(solution)/shard_map/while/body/eval_jaxpr/all_gather | solution.py:29
  221.7 16.1 %gather_fusion = f32[4096,256]{1,0:T(8,128)} fusion(f32[512,256]{1,0:T(8,128)S(1)} %get-tuple-element.454, s32[4096]{0:T(1024)S(1)} %broadcast_clamp_fusion.2), kind=kCustom, calls=%fused_computation.clone.1 | custom fusion | bytes 8404992 | tf_op jit(solution)/shard_map/while/body/eval_jaxpr/gather | solution.py:13
  237.8 5.9 %copy.29 = f32[128,32,256]{0,1,2:T(8,128)} copy(f32[128,32,256]{2,1,0:T(8,128)} %bitcast.60) | data formatting | bytes 8388608 | tf_op jit(solution)/shard_map/while/body/eval_jaxpr/gather | solution.py:13
  243.8 5.5 %fusion.24 = bf16[128,8,256]{0,1,2:T(8,128)(2,1)S(1)} fusion(f32[128,32,256]{0,1,2:T(8,128)} %copy.29, f32[8,32,256]{1,0,2:T(8,128)S(1)} %get-tuple-element.477, f32[128,8]{0,1:T(8,128)S(1)} %fusion.23), kind=kOutput, calls=%fused_computation.4.clone.1 | convolution fusion | flops 101187584 | bytes 4984832 | tf_op jit(solution)/shard_map/while/body/eval_jaxpr/bos,aos->bas/dot_general | solution.py:14
  249.2 5.8 %convolution_bitcast_fusion.2 = f32[128,2048]{1,0:T(8,128)} fusion(bf16[128,8,256]{0,1,2:T(8,128)(2,1)S(1)} %fusion.24, bf16[8,256,2048]{2,0,1:T(8,128)(2,1)} %get-tuple-element.478), kind=kOutput, calls=%fused_computation.1.clone.1 | convolution fusion | flops 1073741824 | bytes 9961472 | tf_op jit(solution)/shard_map/while/body/eval_jaxpr/dot_general | solution.py:24
  255.0 30.5 %reduce-scatter.2.cloned.1.call-done = f32[128,256]{1,0:T(8,128)} async-done(((f32[128,2048]{1,0:T(8,128)}), f32[128,256]{1,0:T(8,128)}) %reduce-scatter.2.cloned.1.call-update) | async-done | bytes 131088 | tf_op jit(solution)/shard_map/while/body/eval_jaxpr/reduce_scatter | solution.py:25
  285.5 1.8 bitcast_dynamic-update-slice_fusion.2
  287.4 10.2 %all_gather.42 = f32[512,256]{1,0:T(8,128)S(1)} all-gather(f32[128,256]{1,0:T(8,128)S(1)} %get-tuple-element.435), channel_id=1, replica_groups=mesh['section'=4,'state'=8] {'section'}, dimensions={0}, use_global_device_ids=true | all-gather | bytes 655360 | tf_op jit(solution)/shard_map/while/body/eval_jaxpr/all_gather | solution.py:58
  297.6 0.1 fusion.25
  297.7 9.5 %all-gather.4 = f32[8,1,128]{2,1,0:T(1,128)S(1)} all-gather(f32[1,1,128]{2,1,0:T(1,128)S(1)} %bitcast.63), channel_id=2, replica_groups=mesh['section'=4,'state'=8] {'state'}, dimensions={0}, use_global_device_ids=true | all-gather | bytes 4608 | tf_op jit(solution)/shard_map/while/body/eval_jaxpr/all_gather | solution.py:29
  307.6 16.1 %gather_fusion = f32[4096,256]{1,0:T(8,128)} fusion(f32[512,256]{1,0:T(8,128)S(1)} %get-tuple-element.454, s32[4096]{0:T(1024)S(1)} %broadcast_clamp_fusion.2), kind=kCustom, calls=%fused_computation.clone.1 | custom fusion | bytes 8404992 | tf_op jit(solution)/shard_map/while/body/eval_jaxpr/gather | solution.py:13
  323.7 5.9 %copy.29 = f32[128,32,256]{0,1,2:T(8,128)} copy(f32[128,32,256]{2,1,0:T(8,128)} %bitcast.60) | data formatting | bytes 8388608 | tf_op jit(solution)/shard_map/while/body/eval_jaxpr/gather | solution.py:13
  329.7 5.5 %fusion.24 = bf16[128,8,256]{0,1,2:T(8,128)(2,1)S(1)} fusion(f32[128,32,256]{0,1,2:T(8,128)} %copy.29, f32[8,32,256]{1,0,2:T(8,128)S(1)} %get-tuple-element.477, f32[128,8]{0,1:T(8,128)S(1)} %fusion.23), kind=kOutput, calls=%fused_computation.4.clone.1 | convolution fusion | flops 101187584 | bytes 4984832 | tf_op jit(solution)/shard_map/while/body/eval_jaxpr/bos,aos->bas/dot_general | solution.py:14
  335.2 5.8 %convolution_bitcast_fusion.2 = f32[128,2048]{1,0:T(8,128)} fusion(bf16[128,8,256]{0,1,2:T(8,128)(2,1)S(1)} %fusion.24, bf16[8,256,2048]{2,0,1:T(8,128)(2,1)} %get-tuple-element.478), kind=kOutput, calls=%fused_computation.1.clone.1 | convolution fusion | flops 1073741824 | bytes 9961472 | tf_op jit(solution)/shard_map/while/body/eval_jaxpr/dot_general | solution.py:24
  341.0 30.4 %reduce-scatter.2.cloned.1.call-done = f32[128,256]{1,0:T(8,128)} async-done(((f32[128,2048]{1,0:T(8,128)}), f32[128,256]{1,0:T(8,128)}) %reduce-scatter.2.cloned.1.call-update) | async-done | bytes 131088 | tf_op jit(solution)/shard_map/while/body/eval_jaxpr/reduce_scatter | solution.py:25
  371.3 1.8 bitcast_dynamic-update-slice_fusion.2
  373.2 10.0 %all_gather.42 = f32[512,256]{1,0:T(8,128)S(1)} all-gather(f32[128,256]{1,0:T(8,128)S(1)} %get-tuple-element.435), channel_id=1, replica_groups=mesh['section'=4,'state'=8] {'section'}, dimensions={0}, use_global_device_ids=true | all-gather | bytes 655360 | tf_op jit(solution)/shard_map/while/body/eval_jaxpr/all_gather | solution.py:58
  383.2 0.1 fusion.25
  383.3 9.3 %all-gather.4 = f32[8,1,128]{2,1,0:T(1,128)S(1)} all-gather(f32[1,1,128]{2,1,0:T(1,128)S(1)} %bitcast.63), channel_id=2, replica_groups=mesh['section'=4,'state'=8] {'state'}, dimensions={0}, use_global_device_ids=true | all-gather | bytes 4608 | tf_op jit(solution)/shard_map/while/body/eval_jaxpr/all_gather | solution.py:29
  392.6 7.3 %all_to_all.40 = f32[4,1,128]{2,1,0:T(1,128)S(1)} all-to-all(f32[4,1,128]{2,1,0:T(1,128)S(1)} %bitcast.66), channel_id=1, replica_groups=mesh['section'=4,'state'=8] {'section'}, dimensions={0} | all-to-all | bytes 4096 | tf_op jit(solution)/shard_map/all_to_all | solution.py:71
  400.0 3.5 all-to-all-start.1
  403.4 7.3 %all-to-all-done.1 = f32[4,128,256]{2,1,0:T(8,128)S(1)} async-done(((f32[4,128,256]{2,1,0:T(8,128)}), f32[4,128,256]{2,1,0:T(8,128)S(1)}, u32[]{:S(2)}, u32[]{:S(2)}) %all-to-all-start.1) | async-done | bytes 524320 | tf_op jit(solution)/shard_map/all_to_all | solution.py:70
  410.8 0.8 copy.48
  411.6 0.6 copy.49
  (55 shorter events, 2.1 us)
Async XLA Ops:
  9.5 37.1 %all-to-all-start = ((f32[1,512,256]{2,0,1:T(1,128)}), f32[1,512,256]{2,0,1:T(1,128)S(1)}, u32[]{:S(2)}, u32[]{:S(2)}) async-start(f32[1,512,256]{2,0,1:T(1,128)} %copy.17), calls=%async_computation.1 | async-start | bytes 1048576 | tf_op jit(solution)/shard_map/all_to_all | solution.py:44
  27.3 11.3 %copy-start.2 = (s32[1,512,32]{1,2,0:T(8,128)S(1)}, s32[1,512,32]{1,2,0:T(8,128)}, u32[]{:S(2)}) copy-start(s32[1,512,32]{1,2,0:T(8,128)} %param.11) | copy-start | bytes 196612
  27.3 20.2 %copy-start = (f32[512,256]{1,0:T(8,128)S(1)}, f32[512,256]{1,0:T(8,128)}, u32[]{:S(2)}) copy-start(f32[512,256]{1,0:T(8,128)} %param.15) | copy-start | bytes 1572868
  27.3 20.2 %copy-start.1 = (f32[8,256]{1,0:T(8,128)S(1)}, f32[8,256]{1,0:T(8,128)}, u32[]{:S(2)}) copy-start(f32[8,256]{1,0:T(8,128)} %param.14) | copy-start | bytes 24580
  47.6 66.7 %reduce-scatter.2.cloned.1.call-start = ((), (), s32[]{:S(2)}) async-start(), calls=%async_computation.4 | async-start | bytes 1179648 | tf_op jit(solution)/shard_map/while/body/eval_jaxpr/reduce_scatter | solution.py:25
  135.7 64.2 %reduce-scatter.2.cloned.1.call-start = ((), (), s32[]{:S(2)}) async-start(), calls=%async_computation.4 | async-start | bytes 1179648 | tf_op jit(solution)/shard_map/while/body/eval_jaxpr/reduce_scatter | solution.py:25
  221.3 64.2 %reduce-scatter.2.cloned.1.call-start = ((), (), s32[]{:S(2)}) async-start(), calls=%async_computation.4 | async-start | bytes 1179648 | tf_op jit(solution)/shard_map/while/body/eval_jaxpr/reduce_scatter | solution.py:25
  307.2 64.1 %reduce-scatter.2.cloned.1.call-start = ((), (), s32[]{:S(2)}) async-start(), calls=%async_computation.4 | async-start | bytes 1179648 | tf_op jit(solution)/shard_map/while/body/eval_jaxpr/reduce_scatter | solution.py:25
  400.0 10.8 %all-to-all-start.1 = ((f32[4,128,256]{2,1,0:T(8,128)}), f32[4,128,256]{2,1,0:T(8,128)S(1)}, u32[]{:S(2)}, u32[]{:S(2)}) async-start(f32[4,128,256]{2,1,0:T(8,128)} %get-tuple-element.318), calls=%async_computation.2 | async-start | bytes 1048576 | tf_op jit(solution)/shard_map/all_to_all | solution.py:70
Sparse Core Ops, SparseCore 0:
  81.4 32.8 reduce-scatter.1
  169.5 30.3 reduce-scatter.1
  255.2 30.3 reduce-scatter.1
  341.1 30.2 reduce-scatter.1
